TPU v7x, 256 devices: a whole 4x4x8 slice. The times are simulated.
256 devices in a mesh: tok: 16 (over y, x), col: 16 (over z, core).
Axes of the slice: x: 4, y: 4, z: 8, core: 2. Of those that a mesh axis runs over, the one named last changes fastest.
Arguments:
- activations: bfloat16 [32768, 8192], P('tok', 'col'), may hold values from -60 to 60, as said below
- weight: bfloat16 [8192, 8192], P('tok', 'col'), may hold values from -6 to 6
- keep_mask: int32 [8192, 8192], P('tok', 'col'), may hold values from 0 to 1
Outputs:
- new_weight: bfloat16 [8192, 8192], P('tok', 'col')
Inputs may be any that keep to these rules, and one draw needn't show every extreme that they name: activations of calibration tokens.
All inputs are finite; a program needn't handle non-finite values.
Results may differ from a plain program's by a relative error of at most 0.00115.
Values may be sent and summed in bfloat16 or wider, within the bound.
A program may use at most 64 MiB of HBM per device.

v0:
```python
import jax
import jax.numpy as jnp
from jax import lax
from jax.sharding import PartitionSpec as P

B = 1024
ITERS = 4


def per_device(activations, weight, keep_mask):
    highest = lax.Precision.HIGHEST
    n_col = lax.axis_size("col")
    n_tok = lax.axis_size("tok")
    tok_rows = activations.shape[0]
    panel_width = B // n_col
    total_count = tok_rows * n_tok
    partial_panel = lax.dot_general(
        activations,
        lax.all_gather(activations[:, :panel_width], "col", axis=1, tiled=True),
        (((0,), (0,)), ((), ())),
        preferred_element_type=jnp.float32,
    )
    hessian_panel = lax.psum(partial_panel, "tok") / total_count
    block_part = hessian_panel[:panel_width]
    diagonal_block = lax.all_gather(block_part, "col", axis=0, tiled=True)
    identity = jnp.eye(B, dtype=jnp.float32)
    damping = 0.01 * jnp.mean(jnp.diagonal(diagonal_block))
    damped = diagonal_block + damping * identity
    frobenius = jnp.sqrt(jnp.sum(damped * damped))
    col_index = lax.axis_index("col")
    row_ids = col_index * panel_width + lax.iota(jnp.int32, panel_width)
    iterate = (row_ids[:, None] == lax.iota(jnp.int32, B)[None, :]).astype(jnp.float32) / frobenius
    for sweep in range(ITERS):
        if sweep == 0:
            whole = identity / frobenius
        else:
            whole = lax.all_gather(iterate.astype(jnp.bfloat16), "col", axis=0, tiled=True).astype(
                iterate.dtype
            )
        product = jnp.dot(iterate, damped, precision=highest)
        iterate = 2.0 * iterate - jnp.dot(product, whole, precision=highest)
    inverse = lax.all_gather(iterate, "col", axis=0, tiled=True)
    pruned = jnp.where(
        keep_mask[:, :panel_width] == 0, weight[:, :panel_width], jnp.zeros((), jnp.bfloat16)
    )
    pruned_panel = lax.all_gather(pruned, "col", axis=1, tiled=True).astype(jnp.float32)
    factor_rows = jnp.dot(pruned_panel, inverse, precision=highest)
    correction = lax.dot_general(
        factor_rows, hessian_panel, (((1,), (1,)), ((), ())), precision=highest
    )
    kept = keep_mask.astype(jnp.float32)
    return (kept * (weight.astype(jnp.float32) - correction)).astype(jnp.bfloat16)


def solution(mesh):
    return jax.shard_map(
        per_device,
        mesh=mesh,
        in_specs=(P("tok", "col"), P("tok", "col"), P("tok", "col")),
        out_specs=P("tok", "col"),
        check_vma=False,
    )
```

profile of v0, /device:TPU:1, one launch (start us, length us, event | category | flops | bytes accessed | tf_op | source)
XLA Modules:
  0.0 456.3 jit_solution(11155648659330884020)
XLA Ops:
  6.5 0.0 all-gather.10.cloned.1.call-start
  6.5 1.1 slice.14
  7.6 0.9 copy.9
  8.5 0.0 all-gather.10.cloned.1.call-update
  8.5 0.0 all-reduce.2.cloned.1.call-start
  8.6 47.0 %all-gather.10.cloned.1.call-done = bf16[2048,1024]{0,1:T(8,128)(2,1)} async-done(((bf16[2048,64]{0,1:T(8,128)(2,1)}), bf16[2048,1024]{0,1:T(8,128)(2,1)}) %all-gather.10.cloned.1.call-update) | async-done | bytes 4194320 | tf_op jit(solution)/shard_map/all_gather | solution.py:19
  55.5 6.6 %fusion.25 = f32[512,1024]{1,0:T(8,128)} fusion(bf16[2048,512]{1,0:T(8,128)(2,1)} %param.3, bf16[2048,1024]{0,1:T(8,128)(2,1)} %all-gather.10.cloned.1.call-done), kind=kOutput, calls=%fused_computation.37 | convolution fusion | flops 2147483648 | bytes 8388608 | tf_op jit(solution)/shard_map/dot_general | solution.py:17
  62.1 0.0 all-reduce.2.cloned.1.call-update
  62.2 0.0 all-gather.12.cloned.1.call-start
  62.2 97.5 %all-reduce.2.cloned.1.call-done = f32[512,1024]{1,0:T(8,128)} async-done(((f32[512,1024]{1,0:T(8,128)}), f32[512,1024]{1,0:T(8,128)}) %all-reduce.2.cloned.1.call-update) | async-done | bytes 2097168 | tf_op jit(solution)/shard_map/psum | solution.py:23
  159.7 1.8 broadcast_multiply_fusion
  161.5 0.7 slice.18
  162.2 0.0 all-gather.12.cloned.1.call-update
  162.3 0.0 all-gather.14.cloned.1.call-start
  162.3 43.1 %all-gather.12.cloned.1.call-done = f32[1024,1024]{1,0:T(8,128)} async-done(((f32[64,1024]{1,0:T(8,128)}), f32[1024,1024]{1,0:T(8,128)}) %all-gather.12.cloned.1.call-update) | async-done | bytes 4194320 | tf_op jit(solution)/shard_map/all_gather | solution.py:25
  205.5 17.2 %gather_fusion = f32[1024]{0:T(1024)S(1)} fusion(f32[1024,1024]{1,0:T(8,128)} %all-gather.12.cloned.1.call-done, s32[1024]{0:T(1024)S(1)} %bitcast.16), kind=kCustom, calls=%fused_computation | custom fusion | bytes 16384 | tf_op jit(solution)/shard_map/jit(diagonal)/cond/branch_0_fun/gather | solution.py:27
  222.7 0.6 reduce_sum.18
  223.9 3.9 multiply_reduce_fusion
  228.5 4.9 %fusion.9 = f32[64,1024]{1,0:T(8,128)S(1)} fusion(f32[1024,1024]{1,0:T(8,128)} %all-gather.12.cloned.1.call-done, f32[]{:T(128)S(6)} %mul_shard_map.3, f32[]{:T(128)S(6)} %sqrt.3, s32[64]{0:T(128)S(1)} %iota_add_fusion), kind=kOutput, calls=%fused_computation.14 | convolution fusion | flops 808583168 | bytes 4456712 | tf_op jit(solution)/shard_map/dot_general | solution.py:40
  233.4 1.9 fusion.22
  235.3 0.0 all-gather.14.cloned.1.call-update
  235.3 0.0 all-gather.16.cloned.1.call-start
  235.4 4.9 %fusion.8 = f32[64,1024]{1,0:T(8,128)S(1)} fusion(f32[64,1024]{1,0:T(8,128)S(1)} %get-tuple-element.6, f32[1024,1024]{1,0:T(8,128)} %all-gather.12.cloned.1.call-done, f32[]{:T(128)S(6)} %mul_shard_map.3), kind=kOutput, calls=%fused_computation.13 | convolution fusion | flops 808452096 | bytes 4718596 | tf_op jit(solution)/shard_map/dot_general | solution.py:40
  240.3 33.5 %all-gather.14.cloned.1.call-done = bf16[1024,1024]{1,0:T(8,128)(2,1)} async-done(((bf16[64,1024]{1,0:T(8,128)(2,1)}), bf16[1024,1024]{1,0:T(8,128)(2,1)}) %all-gather.14.cloned.1.call-update) | async-done | bytes 2097168 | tf_op jit(solution)/shard_map/all_gather | solution.py:37
  273.8 3.5 fusion.23
  277.3 0.0 all-gather.16.cloned.1.call-update
  277.3 0.2 all-gather.18.cloned.1.call-start
  277.5 0.0 slice-start
  277.5 0.0 slice-start.1
  277.5 4.9 %fusion.7 = f32[64,1024]{1,0:T(8,128)S(1)} fusion(f32[64,1024]{1,0:T(8,128)S(1)} %get-tuple-element.8, f32[1024,1024]{1,0:T(8,128)} %all-gather.12.cloned.1.call-done, f32[]{:T(128)S(6)} %mul_shard_map.3), kind=kOutput, calls=%fused_computation.12 | convolution fusion | flops 808452096 | bytes 4718596 | tf_op jit(solution)/shard_map/dot_general | solution.py:40
  282.5 33.0 %all-gather.16.cloned.1.call-done = bf16[1024,1024]{1,0:T(8,128)(2,1)} async-done(((bf16[64,1024]{1,0:T(8,128)(2,1)}), bf16[1024,1024]{1,0:T(8,128)(2,1)}) %all-gather.16.cloned.1.call-update) | async-done | bytes 2097168 | tf_op jit(solution)/shard_map/all_gather | solution.py:37
  315.5 3.5 fusion.24
  318.9 0.0 all-gather.18.cloned.1.call-update
  319.0 0.0 all-gather.8.cloned.1.call-start
  319.0 0.0 slice-done
  319.0 0.1 copy.7
  319.1 0.0 slice-done.1
  319.1 0.1 copy.8
  319.3 0.6 compare_select_fusion
  319.9 0.0 all-gather.8.cloned.1.call-update
  319.9 0.0 all-gather.20.cloned.1.call-start
  320.0 4.9 %fusion.6 = f32[64,1024]{1,0:T(8,128)S(1)} fusion(f32[64,1024]{1,0:T(8,128)S(1)} %get-tuple-element.10, f32[1024,1024]{1,0:T(8,128)} %all-gather.12.cloned.1.call-done, f32[]{:T(128)S(6)} %mul_shard_map.3), kind=kOutput, calls=%fused_computation.11 | convolution fusion | flops 808452096 | bytes 4718596 | tf_op jit(solution)/shard_map/dot_general | solution.py:40
  324.9 32.3 %all-gather.18.cloned.1.call-done = bf16[1024,1024]{1,0:T(8,128)(2,1)} async-done(((bf16[64,1024]{1,0:T(8,128)(2,1)}), bf16[1024,1024]{1,0:T(8,128)(2,1)}) %all-gather.18.cloned.1.call-update) | async-done | bytes 2097168 | tf_op jit(solution)/shard_map/all_gather | solution.py:37
  357.2 3.5 convolution_subtract_fusion.1
  360.7 0.0 copy-start
  360.7 0.0 copy-start.1
  360.7 0.0 all-gather.20.cloned.1.call-update
  360.7 35.4 %all-gather.8.cloned.1.call-done = bf16[512,1024]{0,1:T(8,128)(2,1)} async-done(((bf16[512,64]{0,1:T(8,128)(2,1)}), bf16[512,1024]{0,1:T(8,128)(2,1)}) %all-gather.8.cloned.1.call-update) | async-done | bytes 1048592 | tf_op jit(solution)/shard_map/all_gather | solution.py:46
  396.1 42.8 %all-gather.20.cloned.1.call-done = f32[1024,1024]{1,0:T(8,128)} async-done(((f32[64,1024]{1,0:T(8,128)}), f32[1024,1024]{1,0:T(8,128)}) %all-gather.20.cloned.1.call-update) | async-done | bytes 4194320 | tf_op jit(solution)/shard_map/all_gather | solution.py:42
  438.9 0.0 copy-start.2
  438.9 6.1 %fusion.26 = f32[512,1024]{1,0:T(8,128)S(1)} fusion(bf16[512,1024]{0,1:T(8,128)(2,1)} %all-gather.8.cloned.1.call-done, f32[1024,1024]{1,0:T(8,128)} %all-gather.20.cloned.1.call-done), kind=kOutput, calls=%fused_computation.38 | convolution fusion | flops 6442450944 | bytes 7340032 | tf_op jit(solution)/shard_map/dot_general | solution.py:47
  445.0 0.0 copy-done
  445.0 0.0 copy-done.1
  445.0 0.0 copy-done.2
  445.0 4.5 fusion.5
  (2 shorter events, 0.0 us)
Async XLA Ops:
  6.5 49.0 %all-gather.10.cloned.1.call-start = ((), (), s32[]{:S(2)}) async-start(), calls=%async_computation.1 | async-start | bytes 4456448 | tf_op jit(solution)/shard_map/all_gather | solution.py:19
  8.5 151.2 %all-reduce.2.cloned.1.call-start = ((), (), s32[]{:S(2)}) async-start(), calls=%async_computation.2 | async-start | bytes 4194304 | tf_op jit(solution)/shard_map/psum | solution.py:23
  62.2 143.3 %all-gather.12.cloned.1.call-start = ((), (), s32[]{:S(2)}) async-start(), calls=%async_computation.3 | async-start | bytes 4456448 | tf_op jit(solution)/shard_map/all_gather | solution.py:25
  162.3 111.5 %all-gather.14.cloned.1.call-start = ((), (), s32[]{:S(2)}) async-start(), calls=%async_computation.4 | async-start | bytes 2228224 | tf_op jit(solution)/shard_map/all_gather | solution.py:37
  235.3 80.1 %all-gather.16.cloned.1.call-start = ((), (), s32[]{:S(2)}) async-start(), calls=%async_computation.5 | async-start | bytes 2228224 | tf_op jit(solution)/shard_map/all_gather | solution.py:37
  277.3 79.9 %all-gather.18.cloned.1.call-start = ((), (), s32[]{:S(2)}) async-start(), calls=%async_computation.6 | async-start | bytes 2228224 | tf_op jit(solution)/shard_map/all_gather | solution.py:37
  277.5 41.5 %slice-start = ((s32[512,512]{1,0:T(8,128)}), s32[512,64]{1,0:T(8,128)S(1)}, s32[]{:S(2)}) async-start(s32[512,512]{1,0:T(8,128)} %param.5), calls=%async_computation.8 | async-start | bytes 524288 | tf_op jit(solution)/shard_map/slice | solution.py:44
  277.5 41.6 %slice-start.1 = ((bf16[512,512]{1,0:T(8,128)(2,1)}), bf16[512,64]{1,0:T(8,128)(2,1)S(1)}, s32[]{:S(2)}) async-start(bf16[512,512]{1,0:T(8,128)(2,1)} %param.4), calls=%async_computation.9 | async-start | bytes 262144 | tf_op jit(solution)/shard_map/slice | solution.py:44
  319.0 77.2 %all-gather.8.cloned.1.call-start = ((), (), s32[]{:S(2)}) async-start(), calls=%async_computation | async-start | bytes 1114112 | tf_op jit(solution)/shard_map/all_gather | solution.py:46
  319.9 119.0 %all-gather.20.cloned.1.call-start = ((), (), s32[]{:S(2)}) async-start(), calls=%async_computation.7 | async-start | bytes 4456448 | tf_op jit(solution)/shard_map/all_gather | solution.py:42
  360.7 84.3 %copy-start = (f32[512,1024]{1,0:T(8,128)S(1)}, f32[512,1024]{1,0:T(8,128)}, u32[]{:S(2)}) copy-start(f32[512,1024]{1,0:T(8,128)} %all-reduce.2.cloned.1.call-done) | copy-start | bytes 6291460
  360.7 84.3 %copy-start.1 = (s32[512,512]{1,0:T(8,128)S(1)}, s32[512,512]{1,0:T(8,128)}, u32[]{:S(2)}) copy-start(s32[512,512]{1,0:T(8,128)} %param.5) | copy-start | bytes 3145732
  438.9 6.1 %copy-start.2 = (bf16[512,512]{1,0:T(8,128)(2,1)S(1)}, bf16[512,512]{1,0:T(8,128)(2,1)}, u32[]{:S(2)}) copy-start(bf16[512,512]{1,0:T(8,128)(2,1)} %param.4) | copy-start | bytes 1572868
Sparse Core Ops, SparseCore 0:
  9.2 46.3 all-gather.9
  62.3 97.4 all-reduce.1
  162.4 43.0 all-gather.11
  235.5 38.2 all-gather.13
  277.4 38.0 all-gather.15
  319.1 38.0 all-gather.17
  359.1 36.9 all-gather.7
  398.1 40.7 all-gather.19
where the time goes:
time: 457 us; the launch traced here: 456 us
  waiting for transfers between devices  365 us (80%)
  matrix products  49.1 us (11%)
  local copies, waits for them, and re-layouts  20.1 us (4%)
  between operations  15 us (3%)
  other arithmetic  6.89 us (2%)
    all_gather x3, waiting for transfers between devices, per_device(): lax.all_gather(iterate.astype(jnp.bfloat16), 'col', axis=0, tiled=True)  98.8 us
    psum x1, waiting for transfers between devices, per_device(): hessian_panel = lax.psum(partial_panel, 'tok') / total_count  97.5 us
    all_gather x1, waiting for transfers between devices, per_device(): lax.all_gather(activations[:, :panel_width], 'col', axis=1, tiled=True)  47 us
    all_gather x1, waiting for transfers between devices, per_device(): diagonal_block = lax.all_gather(block_part, 'col', axis=0, tiled=True)  43.1 us
    all_gather x1, waiting for transfers between devices, per_device(): inverse = lax.all_gather(iterate, 'col', axis=0, tiled=True)  42.8 us
    all_gather x1, waiting for transfers between devices, per_device(): lax.all_gather(pruned, 'col', axis=1, tiled=True).astype(jnp.float32)  35.4 us
    dot_general x4, matrix products, per_device(): product = jnp.dot(iterate, damped, precision=highest)  19.6 us
    gather x1, local copies, waits for them, and re-layouts, per_device(): damping = 0.01 * jnp.mean(jnp.diagonal(diagonal_block))  17.2 us
  transfers between devices with their start and end apart: 8, of which 8 were waited for; matrix products, arithmetic and copies ran while one was open for 4% of the time, Pallas kernels for 0%

commit v1 on v0

--- a/solution.py
+++ b/solution.py
@@ -16,7 +16,12 @@
     total_count = tok_rows * n_tok
     partial_panel = lax.dot_general(
         activations,
-        lax.all_gather(activations[:, :panel_width], "col", axis=1, tiled=True),
+        jnp.concatenate(
+            lax.all_to_all(
+                jnp.stack([activations[:, :panel_width]] * lax.axis_size("col")), "col", 0, 0
+            ),
+            axis=1,
+        ),
         (((0,), (0,)), ((), ())),
         preferred_element_type=jnp.float32,
     )

time: 457 us -> 512 us (1.12)
  blocking collectives: 0 us -> 106 us
  waiting for transfers between devices: 365 us -> 316 us
    all_to_all x0 -> x1, blocking collectives: none -> 106 us  [per_device(): lax.all_to_all(jnp.stack([activations[:, :panel_width]] * lax.axis_size('...]
    all_gather x1 -> x0, waiting for transfers between devices: 47 us -> none  [per_device(): lax.all_gather(activations[:, :panel_width], 'col', axis=1, tiled=True)]
  transfers between devices with their start and end apart: 8 -> 7, of which waited for: 8 -> 7; matrix products, arithmetic and copies ran while one was open for 4% -> 4% of each run, Pallas kernels for 0% -> 0%
where the time goes in v1:
time: 512 us; the launch traced here: 511 us
  waiting for transfers between devices  316 us (62%)
  blocking collectives  106 us (21%)
  matrix products  46.2 us (9%)
  local copies, waits for them, and re-layouts  20 us (4%)
  between operations  15 us (3%)
  other arithmetic  6.89 us (1%)
    all_to_all x1, blocking collectives, per_device(): lax.all_to_all(jnp.stack([activations[:, :panel_width]] * lax.axis_size('...  106 us
    all_gather x3, waiting for transfers between devices, per_device(): lax.all_gather(iterate.astype(jnp.bfloat16), 'col', axis=0, tiled=True)  98.8 us
    psum x1, waiting for transfers between devices, per_device(): hessian_panel = lax.psum(partial_panel, 'tok') / total_count  96.1 us
    all_gather x1, waiting for transfers between devices, per_device(): diagonal_block = lax.all_gather(block_part, 'col', axis=0, tiled=True)  43.1 us
    all_gather x1, waiting for transfers between devices, per_device(): inverse = lax.all_gather(iterate, 'col', axis=0, tiled=True)  42.8 us
    all_gather x1, waiting for transfers between devices, per_device(): lax.all_gather(pruned, 'col', axis=1, tiled=True).astype(jnp.float32)  35.2 us
    dot_general x4, matrix products, per_device(): product = jnp.dot(iterate, damped, precision=highest)  19.6 us
    gather x1, local copies, waits for them, and re-layouts, per_device(): damping = 0.01 * jnp.mean(jnp.diagonal(diagonal_block))  17.3 us
  transfers between devices with their start and end apart: 7, of which 7 were waited for; matrix products, arithmetic and copies ran while one was open for 4% of the time, Pallas kernels for 0%

profile of v1, /device:TPU:1, one launch (start us, length us, event | category | flops | bytes accessed | tf_op | source)
XLA Modules:
  0.0 510.5 jit_solution(8288772577103414900)
XLA Ops:
  6.5 0.0 all-reduce.2.cloned.1.call-start
  6.5 1.1 slice.14
  7.6 0.2 copy.7
  7.8 0.5 stack.2
  8.3 0.0 copy-start.3
  8.3 105.9 %all_to_all.5 = bf16[16,2048,64]{1,2,0:T(8,128)(2,1)S(1)} all-to-all(bf16[16,2048,64]{1,2,0:T(8,128)(2,1)S(1)} %stack.2), channel_id=1, replica_groups=mesh['tok'=16,'col'=16] {'col'}, dimensions={0} | all-to-all | bytes 8388608 | tf_op jit(solution)/shard_map/all_to_all | solution.py:20
  114.2 0.0 copy-done.3
  114.2 3.7 fusion.25
  117.9 0.0 all-reduce.2.cloned.1.call-update
  118.0 0.0 all-gather.9.cloned.1.call-start
  118.0 96.1 %all-reduce.2.cloned.1.call-done = f32[512,1024]{1,0:T(8,128)} async-done(((f32[512,1024]{1,0:T(8,128)}), f32[512,1024]{1,0:T(8,128)}) %all-reduce.2.cloned.1.call-update) | async-done | bytes 2097168 | tf_op jit(solution)/shard_map/psum | solution.py:28
  214.1 1.8 broadcast_multiply_fusion
  215.9 0.7 slice.18
  216.6 0.0 all-gather.9.cloned.1.call-update
  216.6 0.0 all-gather.11.cloned.1.call-start
  216.7 43.1 %all-gather.9.cloned.1.call-done = f32[1024,1024]{1,0:T(8,128)} async-done(((f32[64,1024]{1,0:T(8,128)}), f32[1024,1024]{1,0:T(8,128)}) %all-gather.9.cloned.1.call-update) | async-done | bytes 4194320 | tf_op jit(solution)/shard_map/all_gather | solution.py:30
  259.8 17.3 %gather_fusion = f32[1024]{0:T(1024)S(1)} fusion(f32[1024,1024]{1,0:T(8,128)} %all-gather.9.cloned.1.call-done, s32[1024]{0:T(1024)S(1)} %bitcast.19), kind=kCustom, calls=%fused_computation | custom fusion | bytes 16384 | tf_op jit(solution)/shard_map/jit(diagonal)/cond/branch_0_fun/gather | solution.py:32
  277.1 0.6 reduce_sum.18
  278.3 3.9 multiply_reduce_fusion
  282.9 4.9 fusion.9
  287.9 1.9 fusion.22
  289.7 0.0 all-gather.11.cloned.1.call-update
  289.8 0.0 all-gather.13.cloned.1.call-start
  289.8 4.9 fusion.8
  294.7 33.5 %all-gather.11.cloned.1.call-done = bf16[1024,1024]{1,0:T(8,128)(2,1)} async-done(((bf16[64,1024]{1,0:T(8,128)(2,1)}), bf16[1024,1024]{1,0:T(8,128)(2,1)}) %all-gather.11.cloned.1.call-update) | async-done | bytes 2097168 | tf_op jit(solution)/shard_map/all_gather | solution.py:42
  328.2 3.5 fusion.23
  331.7 0.0 all-gather.13.cloned.1.call-update
  331.7 0.2 all-gather.15.cloned.1.call-start
  331.9 0.0 slice-start
  331.9 0.0 slice-start.1
  332.0 4.9 fusion.7
  336.9 33.0 %all-gather.13.cloned.1.call-done = bf16[1024,1024]{1,0:T(8,128)(2,1)} async-done(((bf16[64,1024]{1,0:T(8,128)(2,1)}), bf16[1024,1024]{1,0:T(8,128)(2,1)}) %all-gather.13.cloned.1.call-update) | async-done | bytes 2097168 | tf_op jit(solution)/shard_map/all_gather | solution.py:42
  369.9 3.5 fusion.24
  373.4 0.0 all-gather.15.cloned.1.call-update
  373.4 0.0 all-gather.7.cloned.1.call-start
  373.4 0.0 slice-done
  373.4 0.1 copy.8
  373.6 0.0 slice-done.1
  373.6 0.1 copy.9
  373.7 0.6 compare_select_fusion
  374.3 0.0 all-gather.7.cloned.1.call-update
  374.3 0.0 all-gather.17.cloned.1.call-start
  374.4 4.9 fusion.6
  379.3 32.3 %all-gather.15.cloned.1.call-done = bf16[1024,1024]{1,0:T(8,128)(2,1)} async-done(((bf16[64,1024]{1,0:T(8,128)(2,1)}), bf16[1024,1024]{1,0:T(8,128)(2,1)}) %all-gather.15.cloned.1.call-update) | async-done | bytes 2097168 | tf_op jit(solution)/shard_map/all_gather | solution.py:42
  411.6 3.5 convolution_subtract_fusion.1
  415.1 0.0 copy-start
  415.1 0.0 copy-start.1
  415.1 0.0 all-gather.17.cloned.1.call-update
  415.1 35.2 %all-gather.7.cloned.1.call-done = bf16[512,1024]{0,1:T(8,128)(2,1)} async-done(((bf16[512,64]{0,1:T(8,128)(2,1)}), bf16[512,1024]{0,1:T(8,128)(2,1)}) %all-gather.7.cloned.1.call-update) | async-done | bytes 1048592 | tf_op jit(solution)/shard_map/all_gather | solution.py:51
  450.3 42.8 %all-gather.17.cloned.1.call-done = f32[1024,1024]{1,0:T(8,128)} async-done(((f32[64,1024]{1,0:T(8,128)}), f32[1024,1024]{1,0:T(8,128)}) %all-gather.17.cloned.1.call-update) | async-done | bytes 4194320 | tf_op jit(solution)/shard_map/all_gather | solution.py:47
  493.1 0.0 copy-start.2
  493.1 6.1 %fusion.26 = f32[512,1024]{1,0:T(8,128)S(1)} fusion(bf16[512,1024]{0,1:T(8,128)(2,1)} %all-gather.7.cloned.1.call-done, f32[1024,1024]{1,0:T(8,128)} %all-gather.17.cloned.1.call-done), kind=kOutput, calls=%fused_computation.38 | convolution fusion | flops 6442450944 | bytes 7340032 | tf_op jit(solution)/shard_map/dot_general | solution.py:52
  499.2 0.0 copy-done
  499.2 0.0 copy-done.1
  499.2 0.0 copy-done.2
  499.2 4.5 fusion.5
  (2 shorter events, 0.0 us)
Async XLA Ops:
  6.5 207.6 %all-reduce.2.cloned.1.call-start = ((), (), s32[]{:S(2)}) async-start(), calls=%async_computation.2 | async-start | bytes 4194304 | tf_op jit(solution)/shard_map/psum | solution.py:28
  8.3 105.9 %copy-start.3 = (bf16[2048,512]{1,0:T(8,128)(2,1)S(1)}, bf16[2048,512]{1,0:T(8,128)(2,1)}, u32[]{:S(2)}) copy-start(bf16[2048,512]{1,0:T(8,128)(2,1)} %param.3) | copy-start | bytes 6291460
  118.0 141.9 %all-gather.9.cloned.1.call-start = ((), (), s32[]{:S(2)}) async-start(), calls=%async_computation.3 | async-start | bytes 4456448 | tf_op jit(solution)/shard_map/all_gather | solution.py:30
  216.6 111.6 %all-gather.11.cloned.1.call-start = ((), (), s32[]{:S(2)}) async-start(), calls=%async_computation.4 | async-start | bytes 2228224 | tf_op jit(solution)/shard_map/all_gather | solution.py:42
  289.8 80.1 %all-gather.13.cloned.1.call-start = ((), (), s32[]{:S(2)}) async-start(), calls=%async_computation.5 | async-start | bytes 2228224 | tf_op jit(solution)/shard_map/all_gather | solution.py:42
  331.7 79.9 %all-gather.15.cloned.1.call-start = ((), (), s32[]{:S(2)}) async-start(), calls=%async_computation.6 | async-start | bytes 2228224 | tf_op jit(solution)/shard_map/all_gather | solution.py:42
  331.9 41.5 %slice-start = ((s32[512,512]{1,0:T(8,128)}), s32[512,64]{1,0:T(8,128)S(1)}, s32[]{:S(2)}) async-start(s32[512,512]{1,0:T(8,128)} %param.5), calls=%async_computation.8 | async-start | bytes 524288 | tf_op jit(solution)/shard_map/slice | solution.py:49
  331.9 41.6 %slice-start.1 = ((bf16[512,512]{1,0:T(8,128)(2,1)}), bf16[512,64]{1,0:T(8,128)(2,1)S(1)}, s32[]{:S(2)}) async-start(bf16[512,512]{1,0:T(8,128)(2,1)} %param.4), calls=%async_computation.9 | async-start | bytes 262144 | tf_op jit(solution)/shard_map/slice | solution.py:49
  373.4 76.9 %all-gather.7.cloned.1.call-start = ((), (), s32[]{:S(2)}) async-start(), calls=%async_computation.1 | async-start | bytes 1114112 | tf_op jit(solution)/shard_map/all_gather | solution.py:51
  374.3 118.8 %all-gather.17.cloned.1.call-start = ((), (), s32[]{:S(2)}) async-start(), calls=%async_computation.7 | async-start | bytes 4456448 | tf_op jit(solution)/shard_map/all_gather | solution.py:47
  415.1 84.1 %copy-start = (f32[512,1024]{1,0:T(8,128)S(1)}, f32[512,1024]{1,0:T(8,128)}, u32[]{:S(2)}) copy-start(f32[512,1024]{1,0:T(8,128)} %all-reduce.2.cloned.1.call-done) | copy-start | bytes 6291460
  415.1 84.1 %copy-start.1 = (s32[512,512]{1,0:T(8,128)S(1)}, s32[512,512]{1,0:T(8,128)}, u32[]{:S(2)}) copy-start(s32[512,512]{1,0:T(8,128)} %param.5) | copy-start | bytes 3145732
  493.1 6.1 %copy-start.2 = (bf16[512,512]{1,0:T(8,128)(2,1)S(1)}, bf16[512,512]{1,0:T(8,128)(2,1)}, u32[]{:S(2)}) copy-start(bf16[512,512]{1,0:T(8,128)(2,1)} %param.4) | copy-start | bytes 1572868
Sparse Core Ops, SparseCore 0:
  118.1 95.9 all-reduce.1
  216.7 43.0 all-gather.8
  289.9 38.2 all-gather.10
  331.8 38.0 all-gather.12
  373.5 38.0 all-gather.14
  413.4 36.8 all-gather.6
  452.3 40.7 all-gather.16
